TPU v7x, 32 devices: a whole 2x2x4 slice. The times are simulated.
32 devices in a mesh: dp: 4 (over y, x), owner: 8 (over z, core).
Axes of the slice: x: 2, y: 2, z: 4, core: 2. Of those that a mesh axis runs over, the one named last changes fastest.
Arguments:
- sample_rows: bfloat16 [49152, 4096], P(('dp', 'owner')), may hold values from -60 to 60
- start_basis: bfloat16 [4096, 128], P(('dp', 'owner')), may hold values from -0.09375 to 0.09375
Outputs:
- projected: bfloat16 [49152, 128], P(('dp', 'owner'))
- basis: float32 [4096, 128], P(('dp', 'owner'))
All inputs are finite; a program needn't handle non-finite values.
Results may differ from a plain program's by a relative error of at most 0.0056.
Values may be sent and summed in bfloat16 or wider, within the bound.
No kernel may reach another device: no remote copies, remote signals or barrier semaphores. Data moves between devices by JAX's collectives and lax.ppermute only.
A program may use at most 64 MiB of HBM per device.

v0:
```python
import math
import jax
import jax.numpy as jnp
from jax import lax
from jax.sharding import PartitionSpec as P

ITERS = 2


def body(sample_rows, start_basis):
    devices_all = lax.axis_size("dp") * lax.axis_size("owner")
    features = sample_rows.shape[1]
    owned_rows = features // devices_all
    full_start = lax.all_gather(start_basis, ("dp", "owner"), axis=0, tiled=True)
    image = jnp.dot(sample_rows, full_start, preferred_element_type=jnp.float32)
    ortho = jnp.zeros((owned_rows, start_basis.shape[1]), jnp.float32)
    for iteration in range(ITERS):
        image_low = image.astype(jnp.bfloat16)
        whole_term = lax.dot_general(
            sample_rows, image_low, (((0,), (0,)), ((), ())), preferred_element_type=jnp.float32
        )
        sketch = lax.psum(whole_term, ("dp", "owner"))
        gram = lax.dot_general(
            sketch,
            sketch,
            (((0,), (0,)), ((), ())),
            precision=lax.Precision.HIGHEST,
            preferred_element_type=jnp.float32,
        )
        lower = jnp.linalg.cholesky(gram)
        ortho = jax.scipy.linalg.solve_triangular(lower, sketch.T, lower=True).T
        current = ortho.astype(jnp.bfloat16)
        image = jnp.dot(sample_rows, current, preferred_element_type=jnp.float32)
    ortho = lax.dynamic_slice_in_dim(
        ortho, lax.axis_index(("dp", "owner")) * owned_rows, owned_rows, 0
    )
    return (image.astype(jnp.bfloat16), ortho * math.sqrt(features))


def solution(mesh):
    return jax.shard_map(
        body,
        mesh=mesh,
        in_specs=(P(("dp", "owner"), None), P(("dp", "owner"), None)),
        out_specs=(P(("dp", "owner"), None), P(("dp", "owner"), None)),
        check_vma=False,
    )
```

profile of v0, /device:TPU:0, one launch (start us, length us, event | category | flops | bytes accessed | tf_op | source)
XLA Modules:
  0.0 446.1 jit_solution(10812391194538860089)
XLA Ops:
  7.2 0.0 all-gather.2.cloned.1.call-start
  7.2 0.7 all-gather.2.cloned.1.call-update
  7.9 0.0 all-reduce.3.cloned.1.call-start
  7.9 59.6 %all-gather.2.cloned.1.call-done = bf16[4096,128]{1,0:T(8,128)(2,1)} async-done(((bf16[128,128]{1,0:T(8,128)(2,1)}), bf16[4096,128]{1,0:T(8,128)(2,1)}) %all-gather.2.cloned.1.call-update) | async-done | bytes 1048592 | tf_op jit(solution)/shard_map/all_gather | solution.py:14
  67.5 18.1 %convolution_bitcast_fusion.1 = f32[4096,128]{0,1:T(8,128)} fusion(bf16[1536,4096]{1,0:T(8,128)(2,1)} %param.5, bf16[4096,128]{1,0:T(8,128)(2,1)} %all-gather.2.cloned.1.call-done), kind=kOutput, calls=%fused_computation.1 | convolution fusion | flops 3221422080 | bytes 15728640 | tf_op jit(solution)/shard_map/dot_general | solution.py:19
  85.6 0.0 all-reduce.3.cloned.1.call-update
  85.6 0.2 all-reduce.5.cloned.1.call-start
  85.9 133.6 %all-reduce.3.cloned.1.call-done = f32[4096,128]{0,1:T(8,128)} async-done(((f32[4096,128]{0,1:T(8,128)}), f32[4096,128]{0,1:T(8,128)}) %all-reduce.3.cloned.1.call-update) | async-done | bytes 2097168 | tf_op jit(solution)/shard_map/psum | solution.py:22
  219.5 0.0 copy-start.1
  219.5 4.2 fusion.13
  223.7 0.1 copy.4
  223.8 11.7 %cholesky.44 = f32[128,128]{1,0:T(8,128)S(1)} custom-call(f32[128,128]{1,0:T(8,128)S(1)} %fusion.10), custom_call_target="Cholesky" | custom-call | tf_op jit(solution)/shard_map/jit(cholesky)/cholesky | solution.py:30
  235.5 0.6 compare_reduce_fusion.1
  236.2 0.7 fusion.5
  236.8 9.8 %custom-call.6 = f32[1,128,128]{1,2,0:T(8,128)S(1)} custom-call(f32[1,128,128]{2,1,0:T(8,128)S(1)} %fusion.5), custom_call_target="InvertDiagBlocksLowerTriangular" | custom-call | tf_op jit(solution)/shard_map/jit(_solve_triangular)/triangular_solve | solution.py:31
  246.7 0.0 copy-done.1
  246.7 1.9 convolution_convert_fusion
  248.6 15.6 %convolution_bitcast_fusion = f32[4096,128]{0,1:T(8,128)} fusion(bf16[1536,4096]{1,0:T(8,128)(2,1)} %param.5, bf16[128,4096]{1,0:T(8,128)(2,1)S(1)} %convolution_convert_fusion), kind=kOutput, calls=%fused_computation | convolution fusion | flops 3221422080 | bytes 15728640 | tf_op jit(solution)/shard_map/dot_general | solution.py:19
  264.2 0.0 all-reduce.5.cloned.1.call-update
  264.2 133.5 %all-reduce.5.cloned.1.call-done = f32[4096,128]{0,1:T(8,128)} async-done(((f32[4096,128]{0,1:T(8,128)}), f32[4096,128]{0,1:T(8,128)}) %all-reduce.5.cloned.1.call-update) | async-done | bytes 2097168 | tf_op jit(solution)/shard_map/psum | solution.py:22
  397.7 0.0 copy-start
  397.7 4.2 fusion.14
  401.9 0.1 copy.5
  402.1 11.7 %cholesky.55 = f32[128,128]{1,0:T(8,128)S(1)} custom-call(f32[128,128]{1,0:T(8,128)S(1)} %fusion.8), custom_call_target="Cholesky" | custom-call | tf_op jit(solution)/shard_map/jit(cholesky)/cholesky | solution.py:30
  413.8 0.6 compare_reduce_fusion
  414.4 0.7 fusion.6
  415.1 9.8 %custom-call.7 = f32[1,128,128]{1,2,0:T(8,128)S(1)} custom-call(f32[1,128,128]{2,1,0:T(8,128)S(1)} %fusion.6), custom_call_target="InvertDiagBlocksLowerTriangular" | custom-call | tf_op jit(solution)/shard_map/jit(_solve_triangular)/triangular_solve | solution.py:31
  424.9 0.0 copy-done
  424.9 1.9 fusion.1
  426.9 0.0 copy-start.2
  426.9 1.3 copy-done.2
  428.2 8.8 %fusion = bf16[1536,128]{0,1:T(8,128)(2,1)S(1)} fusion(bf16[1536,4096]{1,0:T(8,128)(2,1)} %param.5, f32[128,4096]{1,0:T(8,128)S(1)} %fusion.1), kind=kOutput, calls=%fused_computation.6 | convolution fusion | flops 1611333632 | bytes 15073280 | tf_op jit(solution)/shard_map/dot_general | solution.py:33
  437.0 0.9 copy.6
  438.0 0.8 multiply_bitcast_fusion
  438.8 0.7 copy.7
  (4 shorter events, 0.1 us)
Async XLA Ops:
  7.2 60.4 %all-gather.2.cloned.1.call-start = ((), (), s32[]{:S(2)}) async-start(), calls=%async_computation | async-start | bytes 1081344 | tf_op jit(solution)/shard_map/all_gather | solution.py:14
  7.9 211.6 %all-reduce.3.cloned.1.call-start = ((), (), s32[]{:S(2)}) async-start(), calls=%async_computation.1 | async-start | bytes 4194304 | tf_op jit(solution)/shard_map/psum | solution.py:22
  85.6 312.1 %all-reduce.5.cloned.1.call-start = ((), (), s32[]{:S(2)}) async-start(), calls=%async_computation.2 | async-start | bytes 4194304 | tf_op jit(solution)/shard_map/psum | solution.py:22
  219.5 27.2 %copy-start.1 = (f32[4096,128]{0,1:T(8,128)S(1)}, f32[4096,128]{0,1:T(8,128)}, u32[]{:S(2)}) copy-start(f32[4096,128]{0,1:T(8,128)} %all-reduce.3.cloned.1.call-done) | copy-start | bytes 6291460
  397.7 27.2 %copy-start = (f32[4096,128]{0,1:T(8,128)S(1)}, f32[4096,128]{0,1:T(8,128)}, u32[]{:S(2)}) copy-start(f32[4096,128]{0,1:T(8,128)} %all-reduce.5.cloned.1.call-done) | copy-start | bytes 6291460
  426.9 1.4 copy-start.2
Sparse Core Ops, SparseCore 0:
  11.0 56.5 all-gather.1
  85.7 133.6 all-reduce.2
  264.4 133.3 all-reduce.4
where the time goes:
time: 446 us
  waiting for transfers between devices  327 us (73%)
  matrix products  54.7 us (12%)
  other arithmetic  46.6 us (10%)
  between operations  13.9 us (3%)
    psum x2, waiting for transfers between devices, body(): sketch = lax.psum(whole_term, ('dp', 'owner'))  267 us
    all_gather x1, waiting for transfers between devices, body(): lax.all_gather(start_basis, ('dp', 'owner'), axis=0, tiled=True)  59.6 us
    dot_general x2, matrix products, body(): lax.dot_general(sample_rows, image_low, (((0,), (0,)), ((), ())), preferr...  33.7 us
    another operation x6, other arithmetic, body(): lower = jnp.linalg.cholesky(gram)  24.8 us
    another operation x4, other arithmetic, body(): ortho = jax.scipy.linalg.solve_triangular(lower, sketch.T, lower=True).T  20.9 us
  transfers between devices with their start and end apart: 3, of which 3 were waited for; matrix products, arithmetic and copies ran while one was open for 0% of the time, Pallas kernels for 0%

commit v1 on v0

--- a/solution.py
+++ b/solution.py
@@ -11,7 +11,22 @@
     devices_all = lax.axis_size("dp") * lax.axis_size("owner")
     features = sample_rows.shape[1]
     owned_rows = features // devices_all
-    full_start = lax.all_gather(start_basis, ("dp", "owner"), axis=0, tiled=True)
+    ways, here, hop = (
+        lax.axis_size(("dp", "owner")),
+        lax.axis_index(("dp", "owner")),
+        start_basis.shape[0],
+    )
+    line, have = (start_basis, 1)
+    while have < ways:
+        line = jnp.concatenate(
+            [
+                line,
+                lax.ppermute(line, ("dp", "owner"), [(d, (d - have) % ways) for d in range(ways)]),
+            ],
+            axis=0,
+        )
+        have = 2 * have
+    full_start = jnp.roll(line, here * hop, axis=0)
     image = jnp.dot(sample_rows, full_start, preferred_element_type=jnp.float32)
     ortho = jnp.zeros((owned_rows, start_basis.shape[1]), jnp.float32)
     for iteration in range(ITERS):

time: 446 us -> 432 us (0.969)
  waiting for transfers between devices: 327 us -> 301 us
  starting transfers between devices: 0.3 us -> 8.26 us
    all_gather x1 -> x0, waiting for transfers between devices: 59.6 us -> none  [body(): lax.all_gather(start_basis, ('dp', 'owner'), axis=0, tiled=True)]
    ppermute x0 -> x5, waiting for transfers between devices: none -> 31.9 us  [body(): lax.ppermute(line, ('dp', 'owner'), [(d, (d - have) % ways) for d in rang...]
    ppermute x0 -> x5, starting transfers between devices: none -> 8 us  [body(): lax.ppermute(line, ('dp', 'owner'), [(d, (d - have) % ways) for d in rang...]
  transfers between devices with their start and end apart: 3 -> 7, of which waited for: 3 -> 7; matrix products, arithmetic and copies ran while one was open for 0% -> 1% of each run, Pallas kernels for 0% -> 0%
where the time goes in v1:
time: 432 us
  waiting for transfers between devices  301 us (70%)
  matrix products  52.2 us (12%)
  other arithmetic  48.9 us (11%)
  between operations  14.2 us (3%)
  starting transfers between devices  8.26 us (2%)
  local copies, waits for them, and re-layouts  7.45 us (2%)
    psum x2, waiting for transfers between devices, body(): sketch = lax.psum(whole_term, ('dp', 'owner'))  269 us
    ppermute x5, waiting for transfers between devices, body(): lax.ppermute(line, ('dp', 'owner'), [(d, (d - have) % ways) for d in rang...  31.9 us
    dot_general x2, matrix products, body(): lax.dot_general(sample_rows, image_low, (((0,), (0,)), ((), ())), preferr...  31.1 us
    another operation x6, other arithmetic, body(): lower = jnp.linalg.cholesky(gram)  24.8 us
    another operation x4, other arithmetic, body(): ortho = jax.scipy.linalg.solve_triangular(lower, sketch.T, lower=True).T  20.9 us
    dot_general x1, matrix products, body(): image = jnp.dot(sample_rows, current, preferred_element_type=jnp.float32)  8.82 us
  transfers between devices with their start and end apart: 7, of which 7 were waited for; matrix products, arithmetic and copies ran while one was open for 1% of the time, Pallas kernels for 0%

profile of v1, /device:TPU:0, one launch (start us, length us, event | category | flops | bytes accessed | tf_op | source)
XLA Modules:
  0.0 431.7 jit_solution(1256492611274300778)
XLA Ops:
  7.2 0.0 copy-start.3
  7.2 0.0 all-reduce.3.cloned.1.call-start
  7.2 6.5 %collective-permute-start = (bf16[128,128]{1,0:T(8,128)(2,1)}, bf16[128,128]{1,0:T(8,128)(2,1)S(1)}, u32[]{:S(2)}, u32[]{:S(2)}) collective-permute-start(bf16[128,128]{1,0:T(8,128)(2,1)} %param.6), channel_id=1, source_target_pairs={{0,31},{1,0},{2,1},{3,2},{4,3},{5,4},{6,5},{7,6},{8,7},{9,8},{10,9... | collective-permute-start | bytes 98312 | tf_op jit(solution)/shard_map/ppermute | solution.py:24
  13.7 1.9 collective-permute-done
  15.6 0.8 pad_maximum_fusion.2
  16.4 0.6 collective-permute-start.1
  16.9 3.7 collective-permute-done.1
  20.6 0.8 pad_maximum_fusion.1
  21.4 0.1 collective-permute-start.2
  21.5 1.4 constant_dynamic-update-slice_fusion.4
  22.8 7.5 %collective-permute-done.2 = bf16[512,128]{1,0:T(8,128)(2,1)S(1)} collective-permute-done((bf16[512,128]{1,0:T(8,128)(2,1)S(1)}, bf16[512,128]{1,0:T(8,128)(2,1)S(1)}, u32[]{:S(2)}, u32[]{:S(2)}) %collective-permute-start.2) | collective-permute-done | bytes 131104 | tf_op jit(solution)/shard_map/ppermute | solution.py:24
  30.3 0.8 pad_maximum_fusion
  31.1 0.1 collective-permute-start.3
  31.2 0.6 constant_dynamic-update-slice_fusion.3
  31.8 0.6 constant_dynamic-update-slice_fusion.2
  32.4 0.7 constant_dynamic-update-slice_fusion.1
  33.1 6.4 %collective-permute-done.3 = bf16[1024,128]{1,0:T(8,128)(2,1)S(1)} collective-permute-done((bf16[1024,128]{1,0:T(8,128)(2,1)S(1)}, bf16[1024,128]{1,0:T(8,128)(2,1)S(1)}, u32[]{:S(2)}, u32[]{:S(2)}) %collective-permute-start.3) | collective-permute-done | bytes 262176 | tf_op jit(solution)/shard_map/ppermute | solution.py:24
  39.5 0.7 constant_dynamic-update-slice_fusion
  40.2 0.9 collective-permute-start.4
  41.1 12.4 %collective-permute-done.4 = bf16[2048,128]{1,0:T(8,128)(2,1)S(1)} collective-permute-done((bf16[2048,128]{1,0:T(8,128)(2,1)}, bf16[2048,128]{1,0:T(8,128)(2,1)S(1)}, u32[]{:S(2)}, u32[]{:S(2)}) %collective-permute-start.4) | collective-permute-done | bytes 524320 | tf_op jit(solution)/shard_map/ppermute | solution.py:24
  53.5 0.1 constant_dynamic-update-slice_fusion.11
  53.6 0.0 copy-done.3
  53.7 0.1 constant_dynamic-update-slice_fusion.5
  53.8 15.5 %convolution_bitcast_fusion.1 = f32[4096,128]{0,1:T(8,128)} fusion(bf16[1536,4096]{1,0:T(8,128)(2,1)} %param.5, bf16[8192,128]{1,0:T(8,128)(2,1)S(1)} %constant_dynamic-update-slice_fusion.5, s32[]{:T(128)S(6)} %select_n.20), kind=kOutput, calls=%fused_computation.1 | convolution fusion | flops 3221422080 | bytes 28311556 | tf_op jit(solution)/shard_map/dot_general | solution.py:34
  69.3 0.0 all-reduce.3.cloned.1.call-update
  69.3 0.2 all-reduce.5.cloned.1.call-start
  69.6 135.2 %all-reduce.3.cloned.1.call-done = f32[4096,128]{0,1:T(8,128)} async-done(((f32[4096,128]{0,1:T(8,128)}), f32[4096,128]{0,1:T(8,128)}) %all-reduce.3.cloned.1.call-update) | async-done | bytes 2097168 | tf_op jit(solution)/shard_map/psum | solution.py:37
  204.8 0.0 copy-start.1
  204.8 4.2 fusion.18
  209.0 0.1 copy.4
  209.1 11.7 %cholesky.44 = f32[128,128]{1,0:T(8,128)S(1)} custom-call(f32[128,128]{1,0:T(8,128)S(1)} %fusion.13), custom_call_target="Cholesky" | custom-call | tf_op jit(solution)/shard_map/jit(cholesky)/cholesky | solution.py:45
  220.8 0.6 compare_reduce_fusion.1
  221.5 0.7 fusion.8
  222.2 9.8 %custom-call.6 = f32[1,128,128]{1,2,0:T(8,128)S(1)} custom-call(f32[1,128,128]{2,1,0:T(8,128)S(1)} %fusion.8), custom_call_target="InvertDiagBlocksLowerTriangular" | custom-call | tf_op jit(solution)/shard_map/jit(_solve_triangular)/triangular_solve | solution.py:46
  232.0 0.0 copy-done.1
  232.0 1.9 convolution_convert_fusion
  233.9 15.6 %convolution_bitcast_fusion = f32[4096,128]{0,1:T(8,128)} fusion(bf16[1536,4096]{1,0:T(8,128)(2,1)} %param.5, bf16[128,4096]{1,0:T(8,128)(2,1)S(1)} %convolution_convert_fusion), kind=kOutput, calls=%fused_computation | convolution fusion | flops 3221422080 | bytes 15728640 | tf_op jit(solution)/shard_map/dot_general | solution.py:34
  249.5 0.0 all-reduce.5.cloned.1.call-update
  249.6 133.6 %all-reduce.5.cloned.1.call-done = f32[4096,128]{0,1:T(8,128)} async-done(((f32[4096,128]{0,1:T(8,128)}), f32[4096,128]{0,1:T(8,128)}) %all-reduce.5.cloned.1.call-update) | async-done | bytes 2097168 | tf_op jit(solution)/shard_map/psum | solution.py:37
  383.1 0.0 copy-start
  383.1 4.2 fusion.19
  387.3 0.1 copy.5
  387.4 11.7 %cholesky.55 = f32[128,128]{1,0:T(8,128)S(1)} custom-call(f32[128,128]{1,0:T(8,128)S(1)} %fusion.11), custom_call_target="Cholesky" | custom-call | tf_op jit(solution)/shard_map/jit(cholesky)/cholesky | solution.py:45
  399.2 0.6 compare_reduce_fusion
  399.8 0.7 fusion.9
  400.5 9.8 %custom-call.7 = f32[1,128,128]{1,2,0:T(8,128)S(1)} custom-call(f32[1,128,128]{2,1,0:T(8,128)S(1)} %fusion.9), custom_call_target="InvertDiagBlocksLowerTriangular" | custom-call | tf_op jit(solution)/shard_map/jit(_solve_triangular)/triangular_solve | solution.py:46
  410.3 0.0 copy-done
  410.3 1.9 fusion.1
  412.2 0.0 copy-start.2
  412.2 1.3 copy-done.2
  413.6 8.8 %fusion = bf16[1536,128]{0,1:T(8,128)(2,1)S(1)} fusion(bf16[1536,4096]{1,0:T(8,128)(2,1)} %param.5, f32[128,4096]{1,0:T(8,128)S(1)} %fusion.1), kind=kOutput, calls=%fused_computation.6 | convolution fusion | flops 1611333632 | bytes 15073280 | tf_op jit(solution)/shard_map/dot_general | solution.py:48
  422.4 0.9 copy.6
  423.3 0.8 multiply_bitcast_fusion
  424.2 0.7 copy.7
  (9 shorter events, 0.2 us)
Async XLA Ops:
  7.2 46.5 %copy-start.3 = (bf16[128,128]{1,0:T(8,128)(2,1)S(1)}, bf16[128,128]{1,0:T(8,128)(2,1)}, u32[]{:S(2)}) copy-start(bf16[128,128]{1,0:T(8,128)(2,1)} %param.6) | copy-start | bytes 98308
  7.2 197.6 %all-reduce.3.cloned.1.call-start = ((), (), s32[]{:S(2)}) async-start(), calls=%async_computation | async-start | bytes 4194304 | tf_op jit(solution)/shard_map/psum | solution.py:37
  7.2 8.4 %collective-permute-start = (bf16[128,128]{1,0:T(8,128)(2,1)}, bf16[128,128]{1,0:T(8,128)(2,1)S(1)}, u32[]{:S(2)}, u32[]{:S(2)}) collective-permute-start(bf16[128,128]{1,0:T(8,128)(2,1)} %param.6), channel_id=1, source_target_pairs={{0,31},{1,0},{2,1},{3,2},{4,3},{5,4},{6,5},{7,6},{8,7},{9,8},{10,9... | collective-permute-start | bytes 98312 | tf_op jit(solution)/shard_map/ppermute | solution.py:24
  16.4 4.3 collective-permute-start.1
  21.4 9.0 %collective-permute-start.2 = (bf16[512,128]{1,0:T(8,128)(2,1)S(1)}, bf16[512,128]{1,0:T(8,128)(2,1)S(1)}, u32[]{:S(2)}, u32[]{:S(2)}) collective-permute-start(bf16[512,128]{1,0:T(8,128)(2,1)S(1)} %pad_maximum_fusion.1), channel_id=1, source_target_pairs={{0,28},{1,29},{2,30},{3,31},{4,0},{5,1},{6,2},{7,3},{8,4},{9,5},{1... | collective-permute-start | bytes 393224 | tf_op jit(solution)/shard_map/ppermute | solution.py:24
  31.1 8.4 %collective-permute-start.3 = (bf16[1024,128]{1,0:T(8,128)(2,1)S(1)}, bf16[1024,128]{1,0:T(8,128)(2,1)S(1)}, u32[]{:S(2)}, u32[]{:S(2)}) collective-permute-start(bf16[1024,128]{1,0:T(8,128)(2,1)S(1)} %pad_maximum_fusion), channel_id=1, source_target_pairs={{0,24},{1,25},{2,26},{3,27},{4,28},{5,29},{6,30},{7,31},{8,0},{9,1... | collective-permute-start | bytes 786440 | tf_op jit(solution)/shard_map/ppermute | solution.py:24
  40.2 13.3 %collective-permute-start.4 = (bf16[2048,128]{1,0:T(8,128)(2,1)}, bf16[2048,128]{1,0:T(8,128)(2,1)S(1)}, u32[]{:S(2)}, u32[]{:S(2)}) collective-permute-start(bf16[2048,128]{1,0:T(8,128)(2,1)} %get-tuple-element.6), channel_id=1, source_target_pairs={{0,16},{1,17},{2,18},{3,19},{4,20},{5,21},{6,22},{7,23},{8,24},{9,... | collective-permute-start | bytes 1572872 | tf_op jit(solution)/shard_map/ppermute | solution.py:24
  69.3 313.8 %all-reduce.5.cloned.1.call-start = ((), (), s32[]{:S(2)}) async-start(), calls=%async_computation.1 | async-start | bytes 4194304 | tf_op jit(solution)/shard_map/psum | solution.py:37
  204.8 27.2 %copy-start.1 = (f32[4096,128]{0,1:T(8,128)S(1)}, f32[4096,128]{0,1:T(8,128)}, u32[]{:S(2)}) copy-start(f32[4096,128]{0,1:T(8,128)} %all-reduce.3.cloned.1.call-done) | copy-start | bytes 6291460
  383.1 27.2 %copy-start = (f32[4096,128]{0,1:T(8,128)S(1)}, f32[4096,128]{0,1:T(8,128)}, u32[]{:S(2)}) copy-start(f32[4096,128]{0,1:T(8,128)} %all-reduce.5.cloned.1.call-done) | copy-start | bytes 6291460
  412.2 1.3 copy-start.2
Sparse Core Ops, SparseCore 0:
  69.4 135.2 all-reduce.2
  249.7 133.3 all-reduce.4
